TPU v7x, 128 devices: a whole 4x4x4 slice. The times are simulated.
128 devices in a mesh: chan: 8 (over z, core), rad: 16 (over y, x).
Axes of the slice: x: 4, y: 4, z: 4, core: 2. Of those that a mesh axis runs over, the one named last changes fastest.
Arguments:
- vectors: float32 [1, 2, 104, 512, 512], P(None, None, 'chan', 'rad'), may hold values from -6 to 6
- eigenvectors: float32 [2, 512, 512], replicated, may hold values from -0.1875 to 0.1875
- energies: float32 [512], replicated, may hold values from 0 to 2
- widths: float32 [512], replicated, may hold values from 0 to 1
- shift_energy: float32 [1], replicated, may hold values from 0.5 to 2
- shift_width: float32 [1], replicated, may hold values from 0.5 to 1
- slot_channel: int32 [104], replicated, may hold values from 0 to 103, as said below
- partners: int32 [104, 12], replicated, may hold values from 0 to 103
- multipole: int32 [104, 12], replicated, may hold values from 0 to 3
- counts: int32 [104], replicated, may hold values from 1 to 12, as said below
- angular: float32 [104, 12], replicated, may hold values from -12 to 12
Outputs:
- update: float32 [1, 2, 104, 512, 512], P(None, None, 'chan', 'rad')
Inputs may be any that keep to these rules, and one draw needn't show every extreme that they name: `slot_channel`: a permutation of the channel numbers; slot s belongs to group s // 13. Entries at positions counts[c] and beyond of a channel's lists are ignored.
All inputs are finite; a program needn't handle non-finite values.
Results may differ from a plain program's by a relative error of at most 0.0024.
Values may be sent and summed in bfloat16 or wider, within the bound.
A program may use at most 64 MiB of HBM per device.

v0:
```python
import math

import jax
import jax.numpy as jnp
from jax import lax
from jax.experimental import pallas as pl
from jax.experimental.pallas import tpu as pltpu
from jax.sharding import PartitionSpec as P

F32 = jnp.float32
BF16 = jnp.bfloat16
MESH = pl.DeviceIdType.MESH
POINTS = 512
CHANNELS = 104
GROUP = 13
ORDERS = 4
LINKS = 12
NCHAN = 8
NRAD = 16
DEVICES = NCHAN * NRAD
ROWS = POINTS // NRAD
HALF = POINTS
FULL = 2 * POINTS

spacing = 0.01
first_point = 8.0
angle_ecs = 0.3


def dot(a, b):
    return jnp.dot(a, b, preferred_element_type=F32)


def split(x):
    hi = x.astype(BF16)
    return hi, (x - hi.astype(F32)).astype(BF16)


def complex_product(a, b):
    return (a[0] * b[0] - a[1] * b[1], a[0] * b[1] + a[1] * b[0])


def kernel(
    vec,
    eig,
    energies,
    widths,
    shift_energy,
    shift_width,
    slot_channel,
    slot_of,
    partners,
    multipole,
    counts,
    angular,
    out,
    xin,
    wr,
    wrt,
    wl,
    wlt,
    fac,
    yh,
    yl,
    zh,
    zl,
    a1,
    fb,
    got,
    csend,
    crecv,
    dsend,
    drecv,
    table,
    t1s,
    t1r,
    t2s,
    t2r,
    t3s,
    t3r,
    t4s,
    t4r,
):
    chan = lax.axis_index("chan")
    rad = lax.axis_index("rad")
    has_slot = rad < GROUP
    my_slot = chan * GROUP + rad
    my_block = rad * NCHAN + chan
    plane = rad // 4

    barrier = pltpu.get_barrier_semaphore()

    @pl.loop(0, DEVICES)
    def _(d):
        to_rad = d // NCHAN
        to_chan = d % NCHAN

        @pl.when(d != my_block)
        def _():
            pl.semaphore_signal(barrier, inc=1, device_id=(to_chan, to_rad), device_id_type=MESH)

    pl.semaphore_wait(barrier, DEVICES - 1)

    my_rows = pl.ds(pl.multiple_of(rad * ROWS, ROWS), ROWS)

    @pl.loop(0, NRAD)
    def _(k):
        s = (rad + 1 + k) % NRAD

        @pl.when(jnp.logical_and(s < GROUP, s != rad))
        def _():
            pltpu.make_async_remote_copy(
                src_ref=vec.at[0, :, s],
                dst_ref=xin.at[:, my_rows],
                send_sem=t1s,
                recv_sem=t1r.at[rad],
                device_id=(chan, s),
                device_id_type=MESH,
            ).start()

    @pl.when(has_slot)
    def _():
        pltpu.make_async_copy(vec.at[0, :, rad], xin.at[:, my_rows], t1r.at[rad]).start()

    @pl.loop(0, 4)
    def _(g):
        rows = pl.ds(pl.multiple_of(g * 128, 128), 128)
        low = pl.ds(pl.multiple_of(HALF + g * 128, 128), 128)
        ur = eig[0, rows, :]
        ui = eig[1, rows, :]
        for part, (r, i) in enumerate(zip(split(ur), split(ui))):
            wr[part, rows, 0:HALF] = r
            wr[part, rows, HALF:FULL] = i
            wr[part, low, 0:HALF] = -i
            wr[part, low, HALF:FULL] = r
            wl[part, rows, 0:HALF] = r
            wl[part, rows, HALF:FULL] = -i
            wl[part, low, 0:HALF] = i
            wl[part, low, HALF:FULL] = r
        tr = eig[0, :, rows].T
        ti = eig[1, :, rows].T
        for part, (r, i) in enumerate(zip(split(tr), split(ti))):
            wrt[part, rows, 0:HALF] = r
            wrt[part, rows, HALF:FULL] = i
            wrt[part, low, 0:HALF] = -i
            wrt[part, low, HALF:FULL] = r
            wlt[part, rows, 0:HALF] = r
            wlt[part, rows, HALF:FULL] = -i
            wlt[part, low, 0:HALF] = i
            wlt[part, low, HALF:FULL] = r
        e_row = jnp.broadcast_to(energies[0:1, :], (128, POINTS))
        w_row = jnp.broadcast_to(widths[0:1, :], (128, POINTS))
        e_col = jnp.broadcast_to(energies[0:1, rows], (POINTS, 128)).T
        w_col = jnp.broadcast_to(widths[0:1, rows], (POINTS, 128)).T
        den_real = e_col + e_row - shift_energy[0]
        den_imag = -(w_col + w_row) - shift_width[0]
        modulus = den_real * den_real + den_imag * den_imag
        fac[0, rows, :] = den_real / modulus
        fac[1, rows, :] = -den_imag / modulus

    row = my_block // 4 * 16 + lax.broadcasted_iota(jnp.int32, (16, 128), 0)
    col = my_block % 4 * 128 + lax.broadcasted_iota(jnp.int32, (16, 128), 1)

    def bent(index):
        start = 3 * POINTS // 4
        position = spacing * (index.astype(F32) + first_point)
        edge = spacing * (start + first_point)
        beyond = jnp.maximum(position - edge, 0.0)
        return (jnp.minimum(position, edge) + beyond * math.cos(angle_ecs), beyond * math.sin(angle_ecs))

    upper = bent(jnp.maximum(row, col))
    lower = bent(jnp.minimum(row, col))
    modulus = upper[0] * upper[0] + upper[1] * upper[1]
    inverse = (upper[0] / modulus, -upper[1] / modulus)
    ratio = complex_product(lower, inverse)
    now = inverse
    for order in range(ORDERS):
        table[order, 0] = now[0]
        table[order, 1] = now[1]
        now = complex_product(now, ratio)

    def left_pair(weights, right_h, right_l, m, size):
        rows = pl.ds(pl.multiple_of(m * size, size), size)
        low = pl.ds(pl.multiple_of(HALF + m * size, size), size)
        result = []
        for r in (rows, low):
            h = weights[0, r, :]
            lo = weights[1, r, :]
            result.append(dot(h, right_h[...]) + dot(h, right_l[...]) + dot(lo, right_h[...]))
        return result

    def scaled_left(m):
        size = 256
        rows = pl.ds(pl.multiple_of(m * size, size), size)
        low = pl.ds(pl.multiple_of(HALF + m * size, size), size)
        re, im = left_pair(wlt, yh, yl, m, size)
        z = complex_product((re, im), (fac[0, rows, :], fac[1, rows, :]))
        for r, v in zip((rows, low), z):
            h, lo = split(v)
            zh[r, :] = h
            zl[r, :] = lo

    def store_y(g, y):
        rows = pl.ds(pl.multiple_of(g * 128, 128), 128)
        low = pl.ds(pl.multiple_of(HALF + g * 128, 128), 128)
        h, lo = split(y)
        yh[rows, :] = h[:, 0:HALF]
        yh[low, :] = h[:, HALF:FULL]
        yl[rows, :] = lo[:, 0:HALF]
        yl[low, :] = lo[:, HALF:FULL]

    @pl.when(has_slot)
    def _():
        @pl.loop(0, 4)
        def _(k):
            g = (plane + k) % 4

            @pl.loop(0, 4)
            def _(q):
                src = 4 * g + q
                part = xin.at[:, pl.ds(pl.multiple_of(src * ROWS, ROWS), ROWS)]
                pltpu.make_async_copy(part, part, t1r.at[src]).wait()

            rows = pl.ds(pl.multiple_of(g * 128, 128), 128)
            x = jnp.concatenate([xin[0, rows, :], xin[1, rows, :]], axis=1)
            h, lo = split(x)
            store_y(g, dot(h, wr[0]) + dot(h, wr[1]) + dot(lo, wr[0]))

        @pl.loop(0, 2)
        def _(m):
            scaled_left(m)

        @pl.loop(0, 4)
        def _(k):
            m = (plane + 1 + k) % 4
            rows = pl.ds(pl.multiple_of(m * 128, 128), 128)
            re, im = left_pair(wl, zh, zl, m, 128)
            a1[0, rows, :] = re
            a1[1, rows, :] = im
            h, lo = split(jnp.concatenate([re, im], axis=1))
            f = (dot(h, wrt[0]) + dot(h, wrt[1]) + dot(lo, wrt[0])).astype(BF16)
            for ii in range(8):
                for j in range(4):
                    for ri in range(2):
                        at = HALF * ri + 128 * j
                        fb[32 * m + 4 * ii + j, ri] = f[16 * ii : 16 * ii + 16, at : at + 128]

            @pl.loop(0, 32)
            def _(q):
                d = 32 * m + q

                @pl.when(d == my_block)
                def _():
                    pltpu.make_async_copy(fb.at[d], got.at[my_slot], t2r).start()

                @pl.when(d != my_block)
                def _():
                    pltpu.make_async_remote_copy(
                        src_ref=fb.at[d],
                        dst_ref=got.at[my_slot],
                        send_sem=t2s,
                        recv_sem=t2r,
                        device_id=(d % NCHAN, d // NCHAN),
                        device_id_type=MESH,
                    ).start()

    pltpu.make_async_copy(got, got, t2r).wait()

    @pl.loop(0, CHANNELS)
    def _(k):
        s = (my_slot + 1 + k) % CHANNELS
        c = slot_channel[s]
        live = counts[c]
        re = jnp.zeros((16, 128), F32)
        im = jnp.zeros((16, 128), F32)
        for p in range(LINKS):
            w = jnp.where(p < live, angular[c, p], 0.0)
            order = multipole[c, p]
            t = slot_of[0, partners[c, p]]
            gr = w * table[order, 0]
            gi = w * table[order, 1]
            vr = got[t, 0].astype(F32)
            vi = got[t, 1].astype(F32)
            re = re + (gr * vr - gi * vi)
            im = im + (gr * vi + gi * vr)
        csend[s, 0] = re.astype(BF16)
        csend[s, 1] = im.astype(BF16)

        to_chan = s // GROUP
        to_rad = s % GROUP
        same = to_rad * NCHAN + to_chan == my_block

        @pl.when(same)
        def _():
            pltpu.make_async_copy(csend.at[s], crecv.at[my_block], t3r.at[my_block // 32]).start()

        @pl.when(jnp.logical_not(same))
        def _():
            pltpu.make_async_remote_copy(
                src_ref=csend.at[s],
                dst_ref=crecv.at[my_block],
                send_sem=t3s,
                recv_sem=t3r.at[my_block // 32],
                device_id=(to_chan, to_rad),
                device_id_type=MESH,
            ).start()

    @pl.when(has_slot)
    def _():
        @pl.loop(0, 4)
        def _(k):
            m = (plane + k) % 4
            part = crecv.at[pl.ds(pl.multiple_of(32 * m, 32), 32)]
            pltpu.make_async_copy(part, part, t3r.at[m]).wait()
            cols = []
            for ri in range(2):
                for j in range(4):
                    cols.append(jnp.concatenate([crecv[32 * m + 4 * ii + j, ri] for ii in range(8)], axis=0))
            x = jnp.concatenate(cols, axis=1)
            store_y(m, dot(x, wr[0]) + dot(x, wr[1]))

        @pl.loop(0, 2)
        def _(m):
            scaled_left(m)

        @pl.loop(0, 4)
        def _(k):
            m = (plane + 1 + k) % 4
            rows = pl.ds(pl.multiple_of(m * 128, 128), 128)
            re, im = left_pair(wl, zh, zl, m, 128)
            for ri, v in enumerate((re, im)):
                diff = (a1[ri, rows, :] - v).astype(BF16)
                for q in range(4):
                    dsend[4 * m + q, ri] = diff[ROWS * q : ROWS * q + ROWS, :]

            @pl.loop(0, 4)
            def _(q):
                r = 4 * m + q

                @pl.when(r == rad)
                def _():
                    pltpu.make_async_copy(dsend.at[r], drecv.at[rad], t4r).start()

                @pl.when(r != rad)
                def _():
                    pltpu.make_async_remote_copy(
                        src_ref=dsend.at[r],
                        dst_ref=drecv.at[rad],
                        send_sem=t4s,
                        recv_sem=t4r,
                        device_id=(chan, r),
                        device_id_type=MESH,
                    ).start()

    pltpu.make_async_copy(drecv, drecv, t4r).wait()

    x = jnp.concatenate(
        [drecv[:, 0].reshape(GROUP * ROWS, POINTS), drecv[:, 1].reshape(GROUP * ROWS, POINTS)], axis=1
    )

    @pl.loop(0, 2)
    def _(ri):
        cols = pl.ds(pl.multiple_of(HALF * ri, HALF), HALF)
        u = dot(x, wrt[0, :, cols]) + dot(x, wrt[1, :, cols])
        out[0, ri] = u.reshape(GROUP, ROWS, POINTS)

    @pl.when(has_slot)
    def _():
        a = xin.at[:, pl.ds(0, (GROUP - 1) * ROWS)]
        pltpu.make_async_copy(a, a, t1s).wait()
        b = fb.at[pl.ds(0, DEVICES - 1)]
        pltpu.make_async_copy(b, b, t2s).wait()
        c = csend.at[pl.ds(0, CHANNELS - 1)]
        pltpu.make_async_copy(c, c, t3s).wait()
        d = dsend.at[pl.ds(0, NRAD - 1)]
        pltpu.make_async_copy(d, d, t4s).wait()

    @pl.when(jnp.logical_not(has_slot))
    def _():
        a = xin.at[:, pl.ds(0, GROUP * ROWS)]
        pltpu.make_async_copy(a, a, t1s).wait()
        pltpu.make_async_copy(csend, csend, t3s).wait()


def local(
    vectors,
    eigenvectors,
    energies,
    widths,
    shift_energy,
    shift_width,
    slot_channel,
    partners,
    multipole,
    counts,
    angular,
):
    slot_ids = jnp.arange(CHANNELS, dtype=jnp.int32)
    slot_of = jnp.sum(jnp.where(slot_channel[:, None] == slot_ids[None, :], slot_ids[:, None], 0), axis=0)
    vmem = pl.BlockSpec(memory_space=pltpu.VMEM)
    smem = pl.BlockSpec(memory_space=pltpu.SMEM)
    dma = pltpu.SemaphoreType.DMA
    return pl.pallas_call(
        kernel,
        name="step",
        out_shape=jax.ShapeDtypeStruct(vectors.shape, F32),
        in_specs=[pl.BlockSpec(memory_space=pl.ANY), vmem, vmem, vmem] + [smem] * 8,
        out_specs=vmem,
        scratch_shapes=[
            pltpu.VMEM((2, POINTS, POINTS), F32),
            pltpu.VMEM((2, FULL, FULL), BF16),
            pltpu.VMEM((2, FULL, FULL), BF16),
            pltpu.VMEM((2, FULL, FULL), BF16),
            pltpu.VMEM((2, FULL, FULL), BF16),
            pltpu.VMEM((2, POINTS, POINTS), F32),
            pltpu.VMEM((FULL, POINTS), BF16),
            pltpu.VMEM((FULL, POINTS), BF16),
            pltpu.VMEM((FULL, POINTS), BF16),
            pltpu.VMEM((FULL, POINTS), BF16),
            pltpu.VMEM((2, POINTS, POINTS), F32),
            pltpu.VMEM((DEVICES, 2, 16, 128), BF16),
            pltpu.VMEM((CHANNELS, 2, 16, 128), BF16),
            pltpu.VMEM((CHANNELS, 2, 16, 128), BF16),
            pltpu.VMEM((DEVICES, 2, 16, 128), BF16),
            pltpu.VMEM((NRAD, 2, ROWS, POINTS), BF16),
            pltpu.VMEM((GROUP, 2, ROWS, POINTS), BF16),
            pltpu.VMEM((ORDERS, 2, 16, 128), F32),
            dma,
            dma((NRAD,)),
            dma,
            dma,
            dma,
            dma((4,)),
            dma,
            dma,
        ],
        compiler_params=pltpu.CompilerParams(
            collective_id=0, has_side_effects=True, vmem_limit_bytes=62 * 1024 * 1024
        ),
    )(
        vectors,
        eigenvectors,
        energies.reshape(1, POINTS),
        widths.reshape(1, POINTS),
        shift_energy,
        shift_width,
        slot_channel,
        slot_of.reshape(1, CHANNELS),
        partners,
        multipole,
        counts,
        angular,
    )


def solution(mesh):
    spread = P(None, None, "chan", "rad", None)
    return jax.shard_map(
        local,
        mesh=mesh,
        in_specs=(spread,) + (P(),) * 10,
        out_specs=spread,
        check_vma=False,
    )
```

profile of v0, /device:TPU:1, one launch (start us, length us, event | category | flops | bytes accessed | tf_op | source)
XLA Modules:
  0.0 122.0 jit_solution(2608501622805844726)
XLA Ops:
  1.3 1.3 %select_reduce_fusion = s32[104]{0:T(128)} fusion(s32[104]{0:T(128)} %slot_channel.1), kind=kLoop, calls=%fused_computation | loop fusion | flops 32344 | bytes 832 | tf_op jit(solution)/shard_map/reduce_sum | solution.py:399
  2.6 1.4 %copy.15.partners = s32[104,12]{1,0:T(8,128)} copy(s32[104,12]{0,1:T(8,128)} %param.18) | data formatting | bytes 9984 | tf_op args[7]
  4.0 1.4 %copy.16.multipole = s32[104,12]{1,0:T(8,128)} copy(s32[104,12]{0,1:T(8,128)} %param.19) | data formatting | bytes 9984 | tf_op args[8]
  5.4 1.4 %copy.17.angular = f32[104,12]{1,0:T(8,128)} copy(f32[104,12]{0,1:T(8,128)} %param.21) | data formatting | bytes 9984 | tf_op args[10]
  6.8 112.3 %step.1 = f32[1,2,13,32,512]{4,3,2,1,0:T(8,128)} custom-call(f32[1,2,13,32,512]{4,3,2,1,0:T(8,128)} %vec.1, f32[2,512,512]{2,1,0:T(8,128)} %eig.1, f32[1,512]{1,0:T(1,128)} %bitcast.3, f32[1,512]{1,0:T(1,128)} %bitcast.4, f32[1]{0:T(128)S(6)} %copy.19.shift_energy, f32[1]{0:T(128)S(6)} %copy.20.shift_width, s32[104]{0:T(128)} %slot_channel.1, ...), custom_call_target="tpu_custom_call" | custom-call | tf_op jit(solution)/shard_map/step/pallas_call | solution.py:403
  119.1 2.9 %copy.21 = f32[1,2,13,32,512]{4,3,2,1,0:T(8,128)} copy(f32[1,2,13,32,512]{4,3,2,1,0:T(8,128)} %step.1) | data formatting | bytes 3407872
where the time goes:
time: 123 us; the launch traced here: 122 us
  Pallas kernels  112 us (91%)
  local copies, waits for them, and re-layouts  7.09 us (6%)
  between operations  1.31 us (1%)
  other arithmetic  1.27 us (1%)
    pallas_call x1, Pallas kernels, local(): pl.pallas_call(kernel, name='step', out_shape=jax.ShapeDtypeStruct(vector...  112 us
    unnamed x4, local copies, waits for them, and re-layouts  7.09 us

commit v1 on v0

v1 whole, which is shorter than its diff:
```python
import math

import jax
import jax.numpy as jnp
from jax import lax
from jax.experimental import pallas as pl
from jax.experimental.pallas import tpu as pltpu
from jax.sharding import PartitionSpec as P

F32 = jnp.float32
BF16 = jnp.bfloat16
MESH = pl.DeviceIdType.MESH
POINTS = 512
CHANNELS = 104
GROUP = 13
ORDERS = 4
LINKS = 12
NCHAN = 8
NRAD = 16
DEVICES = NCHAN * NRAD
ROWS = POINTS // NRAD
HALF = POINTS
FULL = 2 * POINTS

spacing = 0.01
first_point = 8.0
angle_ecs = 0.3


def dot(a, b):
    return jnp.dot(a, b, preferred_element_type=F32)


def split(x):
    hi = x.astype(BF16)
    return hi, (x - hi.astype(F32)).astype(BF16)


def complex_product(a, b):
    return (a[0] * b[0] - a[1] * b[1], a[0] * b[1] + a[1] * b[0])


def kernel(
    vec,
    eig,
    energies,
    widths,
    shift_energy,
    shift_width,
    slot_channel,
    slot_of,
    partners_in,
    multipole_in,
    counts,
    angular_in,
    out,
    xin,
    wr,
    wrt,
    wl,
    wlt,
    fac,
    yh,
    yl,
    zh,
    zl,
    a1,
    fb,
    got,
    csend,
    crecv,
    dsend,
    drecv,
    table,
    t1s,
    t1r,
    t2s,
    t2r,
    t3s,
    t3r,
    t4s,
    t4r,
    ready,
    partners,
    multipole,
    angular,
    tab,
):
    chan = lax.axis_index("chan")
    rad = lax.axis_index("rad")
    seat = (rad + 5 * (chan % 2)) % NRAD
    has_slot = jnp.logical_or(seat % 5 != 0, seat == 0)
    my_place = seat - seat // 5
    my_slot = chan * GROUP + my_place

    def place_of(to_chan, to_rad):
        to_seat = (to_rad + 5 * (to_chan % 2)) % NRAD
        return jnp.logical_or(to_seat % 5 != 0, to_seat == 0), to_seat - to_seat // 5

    def rad_of(to_chan, place):
        to_seat = place + jnp.where(place >= 5, 1, 0) + jnp.where(place >= 9, 1, 0)
        return (to_seat + 11 * (to_chan % 2)) % NRAD

    my_block = 32 * ((rad // 4 + rad % 4) % 4) + NCHAN * (rad % 4) + chan
    plane = rad // 4

    my_rows = pl.ds(pl.multiple_of(rad * ROWS, ROWS), ROWS)

    def left_pair(weights, right_h, right_l, m, size):
        rows = pl.ds(pl.multiple_of(m * size, size), size)
        low = pl.ds(pl.multiple_of(HALF + m * size, size), size)
        result = []
        for r in (rows, low):
            h = weights[0, r, :]
            lo = weights[1, r, :]
            result.append(dot(h, right_h[...]) + dot(h, right_l[...]) + dot(lo, right_h[...]))
        return result

    def scaled_left(m):
        size = 256
        rows = pl.ds(pl.multiple_of(m * size, size), size)
        low = pl.ds(pl.multiple_of(HALF + m * size, size), size)
        re, im = left_pair(wlt, yh, yl, m, size)
        z = complex_product((re, im), (fac[0, rows, :], fac[1, rows, :]))
        for r, v in zip((rows, low), z):
            h, lo = split(v)
            zh[r, :] = h
            zl[r, :] = lo

    def store_y(g, y):
        rows = pl.ds(pl.multiple_of(g * 128, 128), 128)
        low = pl.ds(pl.multiple_of(HALF + g * 128, 128), 128)
        h, lo = split(y)
        yh[rows, :] = h[:, 0:HALF]
        yh[low, :] = h[:, HALF:FULL]
        yl[rows, :] = lo[:, 0:HALF]
        yl[low, :] = lo[:, HALF:FULL]

    barrier = pltpu.get_barrier_semaphore()

    def greet():
        @pl.loop(1, NRAD)
        def _(k):
            to_rad = (rad + k) % NRAD
            pl.semaphore_signal(barrier, inc=1, device_id=(chan, to_rad), device_id_type=MESH)

        @pl.loop(1, NCHAN)
        def _(k):
            to_chan = (chan + k) % NCHAN
            pl.semaphore_signal(barrier, inc=1, device_id=(to_chan, rad), device_id_type=MESH)

        pl.semaphore_wait(barrier, NRAD + NCHAN - 2)

        @pl.loop(1, NCHAN)
        def _(k):
            to_chan = (chan + k) % NCHAN
            pl.semaphore_signal(ready, inc=1, device_id=(to_chan, rad), device_id_type=MESH)

    def send_rows():
        @pl.loop(0, NRAD)
        def _(k):
            s = (rad + 1 + k) % NRAD
            taken, place = place_of(chan, s)

            @pl.when(jnp.logical_and(taken, s != rad))
            def _():
                pltpu.make_async_remote_copy(
                    src_ref=vec.at[0, :, place],
                    dst_ref=xin.at[:, my_rows],
                    send_sem=t1s,
                    recv_sem=t1r.at[rad],
                    device_id=(chan, s),
                    device_id_type=MESH,
                ).start()

        @pl.when(has_slot)
        def _():
            pltpu.make_async_copy(vec.at[0, :, my_place], xin.at[:, my_rows], t1r.at[rad]).start()

    def all_ready():
        pl.semaphore_wait(ready, NCHAN - 1)

    def tables():
        return [
            pltpu.make_async_copy(partners_in, partners, tab.at[0]),
            pltpu.make_async_copy(multipole_in, multipole, tab.at[1]),
            pltpu.make_async_copy(angular_in, angular, tab.at[2]),
        ]

    def prepare():
        for copy in tables():
            copy.start()

        @pl.loop(0, 4)
        def _(g):
            rows = pl.ds(pl.multiple_of(g * 128, 128), 128)
            low = pl.ds(pl.multiple_of(HALF + g * 128, 128), 128)
            ur = eig[0, rows, :]
            ui = eig[1, rows, :]
            for part, (r, i) in enumerate(zip(split(ur), split(ui))):
                wr[part, rows, 0:HALF] = r
                wr[part, rows, HALF:FULL] = i
                wr[part, low, 0:HALF] = -i
                wr[part, low, HALF:FULL] = r
                wl[part, rows, 0:HALF] = r
                wl[part, rows, HALF:FULL] = -i
                wl[part, low, 0:HALF] = i
                wl[part, low, HALF:FULL] = r
            tr = eig[0, :, rows].T
            ti = eig[1, :, rows].T
            for part, (r, i) in enumerate(zip(split(tr), split(ti))):
                wrt[part, rows, 0:HALF] = r
                wrt[part, rows, HALF:FULL] = i
                wrt[part, low, 0:HALF] = -i
                wrt[part, low, HALF:FULL] = r
                wlt[part, rows, 0:HALF] = r
                wlt[part, rows, HALF:FULL] = -i
                wlt[part, low, 0:HALF] = i
                wlt[part, low, HALF:FULL] = r
            e_row = jnp.broadcast_to(energies[0:1, :], (128, POINTS))
            w_row = jnp.broadcast_to(widths[0:1, :], (128, POINTS))
            e_col = jnp.broadcast_to(energies[0:1, rows], (POINTS, 128)).T
            w_col = jnp.broadcast_to(widths[0:1, rows], (POINTS, 128)).T
            den_real = e_col + e_row - shift_energy[0]
            den_imag = -(w_col + w_row) - shift_width[0]
            modulus = den_real * den_real + den_imag * den_imag
            fac[0, rows, :] = den_real / modulus
            fac[1, rows, :] = -den_imag / modulus

        row = my_block // 4 * 16 + lax.broadcasted_iota(jnp.int32, (16, 128), 0)
        col = my_block % 4 * 128 + lax.broadcasted_iota(jnp.int32, (16, 128), 1)

        def bent(index):
            start = 3 * POINTS // 4
            position = spacing * (index.astype(F32) + first_point)
            edge = spacing * (start + first_point)
            beyond = jnp.maximum(position - edge, 0.0)
            return (jnp.minimum(position, edge) + beyond * math.cos(angle_ecs), beyond * math.sin(angle_ecs))

        upper = bent(jnp.maximum(row, col))
        lower = bent(jnp.minimum(row, col))
        modulus = upper[0] * upper[0] + upper[1] * upper[1]
        inverse = (upper[0] / modulus, -upper[1] / modulus)
        ratio = complex_product(lower, inverse)
        now = inverse
        for order in range(ORDERS):
            table[order, 0] = now[0]
            table[order, 1] = now[1]
            now = complex_product(now, ratio)

    def first_pass():
        @pl.when(has_slot)
        def _():
            @pl.loop(0, 4)
            def _(k):
                g = (plane + k) % 4

                @pl.loop(0, 4)
                def _(q):
                    src = 4 * g + q
                    part = xin.at[:, pl.ds(pl.multiple_of(src * ROWS, ROWS), ROWS)]
                    pltpu.make_async_copy(part, part, t1r.at[src]).wait()

                rows = pl.ds(pl.multiple_of(g * 128, 128), 128)
                x = jnp.concatenate([xin[0, rows, :], xin[1, rows, :]], axis=1)
                h, lo = split(x)
                store_y(g, dot(h, wr[0]) + dot(h, wr[1]) + dot(lo, wr[0]))

            @pl.loop(0, 2)
            def _(m):
                scaled_left(m)

            @pl.loop(0, 4)
            def _(k):
                m = (plane + 1 + k) % 4
                rows = pl.ds(pl.multiple_of(m * 128, 128), 128)
                re, im = left_pair(wl, zh, zl, m, 128)
                a1[0, rows, :] = re
                a1[1, rows, :] = im
                h, lo = split(jnp.concatenate([re, im], axis=1))
                f = (dot(h, wrt[0]) + dot(h, wrt[1]) + dot(lo, wrt[0])).astype(BF16)
                for ii in range(8):
                    for j in range(4):
                        for ri in range(2):
                            at = HALF * ri + 128 * j
                            fb[32 * m + 4 * ii + j, ri] = f[16 * ii : 16 * ii + 16, at : at + 128]

                @pl.loop(0, 32)
                def _(q):
                    d = 32 * m + q

                    @pl.when(d == my_block)
                    def _():
                        pltpu.make_async_copy(fb.at[d], got.at[my_slot], t2r).start()

                    @pl.when(d != my_block)
                    def _():
                        pltpu.make_async_remote_copy(
                            src_ref=fb.at[d],
                            dst_ref=got.at[my_slot],
                            send_sem=t2s,
                            recv_sem=t2r,
                            device_id=(q % NCHAN, 4 * ((m + 4 - q // NCHAN) % 4) + q // NCHAN),
                            device_id_type=MESH,
                        ).start()

    def couple():
        pltpu.make_async_copy(got, got, t2r).wait()

        @pl.loop(0, CHANNELS)
        def _(k):
            s = (my_slot + 1 + k) % CHANNELS
            c = slot_channel[s]
            live = counts[c]
            re = jnp.zeros((16, 128), F32)
            im = jnp.zeros((16, 128), F32)
            for p in range(LINKS):
                w = jnp.where(p < live, angular[c, p], 0.0)
                order = multipole[c, p]
                t = slot_of[0, partners[c, p]]
                gr = w * table[order, 0]
                gi = w * table[order, 1]
                vr = got[t, 0].astype(F32)
                vi = got[t, 1].astype(F32)
                re = re + (gr * vr - gi * vi)
                im = im + (gr * vi + gi * vr)
            csend[s, 0] = re.astype(BF16)
            csend[s, 1] = im.astype(BF16)

            to_chan = s // GROUP
            to_rad = rad_of(to_chan, s % GROUP)
            same = jnp.logical_and(to_rad == rad, to_chan == chan)

            @pl.when(same)
            def _():
                pltpu.make_async_copy(csend.at[s], crecv.at[my_block], t3r.at[my_block // 32]).start()

            @pl.when(jnp.logical_not(same))
            def _():
                pltpu.make_async_remote_copy(
                    src_ref=csend.at[s],
                    dst_ref=crecv.at[my_block],
                    send_sem=t3s,
                    recv_sem=t3r.at[my_block // 32],
                    device_id=(to_chan, to_rad),
                    device_id_type=MESH,
                ).start()

    def second_pass():
        @pl.when(has_slot)
        def _():
            @pl.loop(0, 4)
            def _(k):
                m = (plane + k) % 4
                part = crecv.at[pl.ds(pl.multiple_of(32 * m, 32), 32)]
                pltpu.make_async_copy(part, part, t3r.at[m]).wait()
                cols = []
                for ri in range(2):
                    for j in range(4):
                        cols.append(jnp.concatenate([crecv[32 * m + 4 * ii + j, ri] for ii in range(8)], axis=0))
                x = jnp.concatenate(cols, axis=1)
                store_y(m, dot(x, wr[0]) + dot(x, wr[1]))

            @pl.loop(0, 2)
            def _(m):
                scaled_left(m)

            @pl.loop(0, 4)
            def _(k):
                m = (plane + 1 + k) % 4
                rows = pl.ds(pl.multiple_of(m * 128, 128), 128)
                re, im = left_pair(wl, zh, zl, m, 128)
                for ri, v in enumerate((re, im)):
                    diff = (a1[ri, rows, :] - v).astype(BF16)
                    for q in range(4):
                        dsend[4 * m + q, ri] = diff[ROWS * q : ROWS * q + ROWS, :]

                @pl.loop(0, 4)
                def _(q):
                    r = 4 * m + q

                    @pl.when(r == rad)
                    def _():
                        pltpu.make_async_copy(dsend.at[r], drecv.at[my_place], t4r).start()

                    @pl.when(r != rad)
                    def _():
                        pltpu.make_async_remote_copy(
                            src_ref=dsend.at[r],
                            dst_ref=drecv.at[my_place],
                            send_sem=t4s,
                            recv_sem=t4r,
                            device_id=(chan, r),
                            device_id_type=MESH,
                        ).start()

    def finish():
        pltpu.make_async_copy(drecv, drecv, t4r).wait()

        x = jnp.concatenate(
            [drecv[:, 0].reshape(GROUP * ROWS, POINTS), drecv[:, 1].reshape(GROUP * ROWS, POINTS)], axis=1
        )

        @pl.loop(0, 2)
        def _(ri):
            cols = pl.ds(pl.multiple_of(HALF * ri, HALF), HALF)
            u = dot(x, wrt[0, :, cols]) + dot(x, wrt[1, :, cols])
            out[0, ri] = u.reshape(GROUP, ROWS, POINTS)

    def drain():
        @pl.when(has_slot)
        def _():
            a = xin.at[:, pl.ds(0, (GROUP - 1) * ROWS)]
            pltpu.make_async_copy(a, a, t1s).wait()
            b = fb.at[pl.ds(0, DEVICES - 1)]
            pltpu.make_async_copy(b, b, t2s).wait()
            c = csend.at[pl.ds(0, CHANNELS - 1)]
            pltpu.make_async_copy(c, c, t3s).wait()
            d = dsend.at[pl.ds(0, NRAD - 1)]
            pltpu.make_async_copy(d, d, t4s).wait()

        @pl.when(jnp.logical_not(has_slot))
        def _():
            a = xin.at[:, pl.ds(0, GROUP * ROWS)]
            pltpu.make_async_copy(a, a, t1s).wait()
            pltpu.make_async_copy(csend, csend, t3s).wait()

    greet()
    send_rows()
    prepare()
    all_ready()
    for copy in tables():
        copy.wait()
    first_pass()
    couple()
    second_pass()
    finish()
    drain()


def local(
    vectors,
    eigenvectors,
    energies,
    widths,
    shift_energy,
    shift_width,
    slot_channel,
    partners,
    multipole,
    counts,
    angular,
):
    slot_ids = jnp.arange(CHANNELS, dtype=jnp.int32)
    slot_of = jnp.sum(jnp.where(slot_channel[:, None] == slot_ids[None, :], slot_ids[:, None], 0), axis=0)
    vmem = pl.BlockSpec(memory_space=pltpu.VMEM)
    smem = pl.BlockSpec(memory_space=pltpu.SMEM)
    anywhere = pl.BlockSpec(memory_space=pl.ANY)
    dma = pltpu.SemaphoreType.DMA
    return pl.pallas_call(
        kernel,
        name="step",
        out_shape=jax.ShapeDtypeStruct(vectors.shape, F32),
        in_specs=[pl.BlockSpec(memory_space=pl.ANY), vmem, vmem, vmem] + [smem] * 4 + [anywhere, anywhere, smem, anywhere],
        out_specs=vmem,
        scratch_shapes=[
            pltpu.VMEM((2, POINTS, POINTS), F32),
            pltpu.VMEM((2, FULL, FULL), BF16),
            pltpu.VMEM((2, FULL, FULL), BF16),
            pltpu.VMEM((2, FULL, FULL), BF16),
            pltpu.VMEM((2, FULL, FULL), BF16),
            pltpu.VMEM((2, POINTS, POINTS), F32),
            pltpu.VMEM((FULL, POINTS), BF16),
            pltpu.VMEM((FULL, POINTS), BF16),
            pltpu.VMEM((FULL, POINTS), BF16),
            pltpu.VMEM((FULL, POINTS), BF16),
            pltpu.VMEM((2, POINTS, POINTS), F32),
            pltpu.VMEM((DEVICES, 2, 16, 128), BF16),
            pltpu.VMEM((CHANNELS, 2, 16, 128), BF16),
            pltpu.VMEM((CHANNELS, 2, 16, 128), BF16),
            pltpu.VMEM((DEVICES, 2, 16, 128), BF16),
            pltpu.VMEM((NRAD, 2, ROWS, POINTS), BF16),
            pltpu.VMEM((GROUP, 2, ROWS, POINTS), BF16),
            pltpu.VMEM((ORDERS, 2, 16, 128), F32),
            dma,
            dma((NRAD,)),
            dma,
            dma,
            dma,
            dma((4,)),
            dma,
            dma,
            pltpu.SemaphoreType.REGULAR,
            pltpu.SMEM((CHANNELS, LINKS), jnp.int32),
            pltpu.SMEM((CHANNELS, LINKS), jnp.int32),
            pltpu.SMEM((CHANNELS, LINKS), F32),
            dma((3,)),
        ],
        compiler_params=pltpu.CompilerParams(
            collective_id=0, has_side_effects=True, vmem_limit_bytes=62 * 1024 * 1024
        ),
    )(
        vectors,
        eigenvectors,
        energies.reshape(1, POINTS),
        widths.reshape(1, POINTS),
        shift_energy,
        shift_width,
        slot_channel,
        slot_of.reshape(1, CHANNELS),
        partners,
        multipole,
        counts,
        angular,
    )


def solution(mesh):
    spread = P(None, None, "chan", "rad", None)
    return jax.shard_map(
        local,
        mesh=mesh,
        in_specs=(spread,) + (P(),) * 10,
        out_specs=spread,
        check_vma=False,
    )
```

time: 123 us -> 115 us (0.935)
  Pallas kernels: 112 us -> 105 us
    pallas_call x1, Pallas kernels: 112 us -> 105 us  [local(): pl.pallas_call(kernel, name='step', out_shape=jax.ShapeDtypeStruct(vector...]
where the time goes in v1:
time: 115 us
  Pallas kernels  105 us (91%)
  local copies, waits for them, and re-layouts  7.09 us (6%)
  between operations  1.31 us (1%)
  other arithmetic  1.27 us (1%)
    pallas_call x1, Pallas kernels, local(): pl.pallas_call(kernel, name='step', out_shape=jax.ShapeDtypeStruct(vector...  105 us
    unnamed x4, local copies, waits for them, and re-layouts  7.09 us

profile of v1, /device:TPU:1, one launch (start us, length us, event | category | flops | bytes accessed | tf_op | source)
XLA Modules:
  0.0 115.0 jit_solution(919906822474943193)
XLA Ops:
  1.3 1.3 %select_reduce_fusion = s32[104]{0:T(128)} fusion(s32[104]{0:T(128)} %slot_channel.1), kind=kLoop, calls=%fused_computation | loop fusion | flops 32344 | bytes 832 | tf_op jit(solution)/shard_map/reduce_sum | solution.py:455
  2.6 1.4 %copy.15.partners_in = s32[104,12]{1,0:T(8,128)} copy(s32[104,12]{0,1:T(8,128)} %param.18) | data formatting | bytes 9984 | tf_op args[7]
  4.0 1.4 %copy.16.multipole_in = s32[104,12]{1,0:T(8,128)} copy(s32[104,12]{0,1:T(8,128)} %param.19) | data formatting | bytes 9984 | tf_op args[8]
  5.4 1.4 %copy.17.angular_in = f32[104,12]{1,0:T(8,128)} copy(f32[104,12]{0,1:T(8,128)} %param.21) | data formatting | bytes 9984 | tf_op args[10]
  6.8 105.3 %step.1 = f32[1,2,13,32,512]{4,3,2,1,0:T(8,128)} custom-call(f32[1,2,13,32,512]{4,3,2,1,0:T(8,128)} %vec.1, f32[2,512,512]{2,1,0:T(8,128)} %eig.1, f32[1,512]{1,0:T(1,128)} %bitcast.3, f32[1,512]{1,0:T(1,128)} %bitcast.4, f32[1]{0:T(128)S(6)} %copy.19.shift_energy, f32[1]{0:T(128)S(6)} %copy.20.shift_width, s32[104]{0:T(128)} %slot_channel.1, ...), custom_call_target="tpu_custom_call" | custom-call | tf_op jit(solution)/shard_map/step/pallas_call | solution.py:460
  112.1 2.9 %copy.21 = f32[1,2,13,32,512]{4,3,2,1,0:T(8,128)} copy(f32[1,2,13,32,512]{4,3,2,1,0:T(8,128)} %step.1) | data formatting | bytes 3407872

commit v2 on v1

--- a/solution.py
+++ b/solution.py
@@ -307,9 +307,7 @@
     def couple():
         pltpu.make_async_copy(got, got, t2r).wait()
 
-        @pl.loop(0, CHANNELS)
-        def _(k):
-            s = (my_slot + 1 + k) % CHANNELS
+        def mixed(s):
             c = slot_channel[s]
             live = counts[c]
             re = jnp.zeros((16, 128), F32)
@@ -324,27 +322,37 @@
                 vi = got[t, 1].astype(F32)
                 re = re + (gr * vr - gi * vi)
                 im = im + (gr * vi + gi * vr)
-            csend[s, 0] = re.astype(BF16)
-            csend[s, 1] = im.astype(BF16)
-
-            to_chan = s // GROUP
-            to_rad = rad_of(to_chan, s % GROUP)
-            same = jnp.logical_and(to_rad == rad, to_chan == chan)
-
-            @pl.when(same)
-            def _():
-                pltpu.make_async_copy(csend.at[s], crecv.at[my_block], t3r.at[my_block // 32]).start()
-
-            @pl.when(jnp.logical_not(same))
-            def _():
-                pltpu.make_async_remote_copy(
-                    src_ref=csend.at[s],
-                    dst_ref=crecv.at[my_block],
-                    send_sem=t3s,
-                    recv_sem=t3r.at[my_block // 32],
-                    device_id=(to_chan, to_rad),
-                    device_id_type=MESH,
-                ).start()
+            return re.astype(BF16), im.astype(BF16)
+
+        @pl.loop(0, CHANNELS // 4)
+        def _(k):
+            slots = [(my_slot + 1 + k + CHANNELS // 4 * u) % CHANNELS for u in range(4)]
+            fields = [mixed(s) for s in slots]
+            for s, (re, im) in zip(slots, fields):
+                csend[s, 0] = re
+                csend[s, 1] = im
+
+            @pl.loop(0, 4)
+            def _(u):
+                s = (my_slot + 1 + k + CHANNELS // 4 * u) % CHANNELS
+                to_chan = s // GROUP
+                to_rad = rad_of(to_chan, s % GROUP)
+                same = jnp.logical_and(to_rad == rad, to_chan == chan)
+
+                @pl.when(same)
+                def _():
+                    pltpu.make_async_copy(csend.at[s], crecv.at[my_block], t3r.at[my_block // 32]).start()
+
+                @pl.when(jnp.logical_not(same))
+                def _():
+                    pltpu.make_async_remote_copy(
+                        src_ref=csend.at[s],
+                        dst_ref=crecv.at[my_block],
+                        send_sem=t3s,
+                        recv_sem=t3r.at[my_block // 32],
+                        device_id=(to_chan, to_rad),
+                        device_id_type=MESH,
+                    ).start()
 
     def second_pass():
         @pl.when(has_slot)
@@ -367,7 +375,7 @@
 
             @pl.loop(0, 4)
             def _(k):
-                m = (plane + 1 + k) % 4
+                m = (plane + jnp.where(k == 1, 3, jnp.where(k == 2, 2, jnp.where(k == 3, 4, 1)))) % 4
                 rows = pl.ds(pl.multiple_of(m * 128, 128), 128)
                 re, im = left_pair(wl, zh, zl, m, 128)
                 for ri, v in enumerate((re, im)):

time: 115 us -> 114 us (level)
    pallas_call x1, Pallas kernels: 105 us -> 104 us  [local(): pl.pallas_call(kernel, name='step', out_shape=jax.ShapeDtypeStruct(vector...]
where the time goes in v2:
time: 114 us; the launch traced here: 113 us
  Pallas kernels  104 us (91%)
  local copies, waits for them, and re-layouts  7.09 us (6%)
  between operations  1.31 us (1%)
  other arithmetic  1.27 us (1%)
    pallas_call x1, Pallas kernels, local(): pl.pallas_call(kernel, name='step', out_shape=jax.ShapeDtypeStruct(vector...  104 us
    unnamed x4, local copies, waits for them, and re-layouts  7.09 us

profile of v2, /device:TPU:1, one launch (start us, length us, event | category | flops | bytes accessed | tf_op | source)
XLA Modules:
  0.0 113.2 jit_solution(16856458116674890237)
XLA Ops:
  1.3 1.3 %select_reduce_fusion = s32[104]{0:T(128)} fusion(s32[104]{0:T(128)} %slot_channel.1), kind=kLoop, calls=%fused_computation | loop fusion | flops 32344 | bytes 832 | tf_op jit(solution)/shard_map/reduce_sum | solution.py:463
  2.6 1.4 %copy.15.partners_in = s32[104,12]{1,0:T(8,128)} copy(s32[104,12]{0,1:T(8,128)} %param.18) | data formatting | bytes 9984 | tf_op args[7]
  4.0 1.4 %copy.16.multipole_in = s32[104,12]{1,0:T(8,128)} copy(s32[104,12]{0,1:T(8,128)} %param.19) | data formatting | bytes 9984 | tf_op args[8]
  5.4 1.4 %copy.17.angular_in = f32[104,12]{1,0:T(8,128)} copy(f32[104,12]{0,1:T(8,128)} %param.21) | data formatting | bytes 9984 | tf_op args[10]
  6.8 103.5 %step.1 = f32[1,2,13,32,512]{4,3,2,1,0:T(8,128)} custom-call(f32[1,2,13,32,512]{4,3,2,1,0:T(8,128)} %vec.1, f32[2,512,512]{2,1,0:T(8,128)} %eig.1, f32[1,512]{1,0:T(1,128)} %bitcast.3, f32[1,512]{1,0:T(1,128)} %bitcast.4, f32[1]{0:T(128)S(6)} %copy.19.shift_energy, f32[1]{0:T(128)S(6)} %copy.20.shift_width, s32[104]{0:T(128)} %slot_channel.1, ...), custom_call_target="tpu_custom_call" | custom-call | tf_op jit(solution)/shard_map/step/pallas_call | solution.py:468
  110.3 2.9 %copy.21 = f32[1,2,13,32,512]{4,3,2,1,0:T(8,128)} copy(f32[1,2,13,32,512]{4,3,2,1,0:T(8,128)} %step.1) | data formatting | bytes 3407872

commit v3 on v2

--- a/solution.py
+++ b/solution.py
@@ -286,7 +286,8 @@
                             fb[32 * m + 4 * ii + j, ri] = f[16 * ii : 16 * ii + 16, at : at + 128]
 
                 @pl.loop(0, 32)
-                def _(q):
+                def _(turn):
+                    q = (turn + my_slot) % 32
                     d = 32 * m + q
 
                     @pl.when(d == my_block)
@@ -384,8 +385,8 @@
                         dsend[4 * m + q, ri] = diff[ROWS * q : ROWS * q + ROWS, :]
 
                 @pl.loop(0, 4)
-                def _(q):
-                    r = 4 * m + q
+                def _(turn):
+                    r = 4 * m + (turn + rad + 1) % 4
 
                     @pl.when(r == rad)
                     def _():

time: 114 us -> 116 us (1.018)
    pallas_call x1, Pallas kernels: 104 us -> 105 us  [local(): pl.pallas_call(kernel, name='step', out_shape=jax.ShapeDtypeStruct(vector...]
where the time goes in v3:
time: 116 us; the launch traced here: 114 us
  Pallas kernels  105 us (91%)
  local copies, waits for them, and re-layouts  7.09 us (6%)
  between operations  1.31 us (1%)
  other arithmetic  1.27 us (1%)
    pallas_call x1, Pallas kernels, local(): pl.pallas_call(kernel, name='step', out_shape=jax.ShapeDtypeStruct(vector...  105 us
    unnamed x4, local copies, waits for them, and re-layouts  7.09 us

profile of v3, /device:TPU:1, one launch (start us, length us, event | category | flops | bytes accessed | tf_op | source)
XLA Modules:
  0.0 114.5 jit_solution(11063919968195842511)
XLA Ops:
  1.3 1.3 %select_reduce_fusion = s32[104]{0:T(128)} fusion(s32[104]{0:T(128)} %slot_channel.1), kind=kLoop, calls=%fused_computation | loop fusion | flops 32344 | bytes 832 | tf_op jit(solution)/shard_map/reduce_sum | solution.py:464
  2.6 1.4 %copy.15.partners_in = s32[104,12]{1,0:T(8,128)} copy(s32[104,12]{0,1:T(8,128)} %param.18) | data formatting | bytes 9984 | tf_op args[7]
  4.0 1.4 %copy.16.multipole_in = s32[104,12]{1,0:T(8,128)} copy(s32[104,12]{0,1:T(8,128)} %param.19) | data formatting | bytes 9984 | tf_op args[8]
  5.4 1.4 %copy.17.angular_in = f32[104,12]{1,0:T(8,128)} copy(f32[104,12]{0,1:T(8,128)} %param.21) | data formatting | bytes 9984 | tf_op args[10]
  6.8 104.8 %step.1 = f32[1,2,13,32,512]{4,3,2,1,0:T(8,128)} custom-call(f32[1,2,13,32,512]{4,3,2,1,0:T(8,128)} %vec.1, f32[2,512,512]{2,1,0:T(8,128)} %eig.1, f32[1,512]{1,0:T(1,128)} %bitcast.3, f32[1,512]{1,0:T(1,128)} %bitcast.4, f32[1]{0:T(128)S(6)} %copy.19.shift_energy, f32[1]{0:T(128)S(6)} %copy.20.shift_width, s32[104]{0:T(128)} %slot_channel.1, ...), custom_call_target="tpu_custom_call" | custom-call | tf_op jit(solution)/shard_map/step/pallas_call | solution.py:469
  111.6 2.9 %copy.21 = f32[1,2,13,32,512]{4,3,2,1,0:T(8,128)} copy(f32[1,2,13,32,512]{4,3,2,1,0:T(8,128)} %step.1) | data formatting | bytes 3407872
